TPU v7x, 256 devices: a whole 4x4x8 slice. The times are simulated.
256 devices in a mesh: shard: 32 (over y, z), blk: 8 (over x, core).
Axes of the slice: x: 4, y: 4, z: 8, core: 2. Of those that a mesh axis runs over, the one named last changes fastest.
Arguments:
- request_embeddings: bfloat16 [65536, 256], P(('shard', 'blk')), may hold values from -0.5 to 0.5
- frequent_entry_matrix: bfloat16 [2048, 256], replicated, may hold values from -0.23925781 to 0.23925781
- rare_entry_matrix: float32 [65536, 256], P('shard'), may hold values from -0.24 to 0.24
- frequent_entry_lines: int32 [65536, 4], P(('shard', 'blk')), may hold values from 0 to 2047
- rare_place_parent: int32 [65536, 4], P(('shard', 'blk')), may hold values from 0 to 31, all different within a row; in each aligned block of 256 rows (0 to 255, 256 to 511, ...) at most 64 rows name the same one
- rare_local_position: int32 [65536, 4], P(('shard', 'blk')), may hold values from 0 to 2047
- rare_place_tally: int32 [65536], P(('shard', 'blk')), may hold values from 1 to 4
- sharpness_factor: float32 [1], replicated, may hold values from 4 to 16
- pairscore_additive: float32 [1], replicated, may hold values from -6 to -2
Outputs:
- request_derivative: float32 [65536, 256], P(('shard', 'blk'))
- hot_grad: float32 [2048, 256], replicated
- cold_grad: float32 [65536, 256], P(('shard', 'blk'))
Inputs may be any that keep to these rules, and one draw needn't show every extreme that they name: `rare_place_parent`: each row names 4 different owners; among the rows of one device no owner is named by more than 64 rows, a bound that some block reaches.
All inputs are finite; a program needn't handle non-finite values.
Results may differ from a plain program's by a relative error of at most 0.007.
Values may be sent and summed in bfloat16 or wider, within the bound.
No kernel may reach another device: no remote copies, remote signals or barrier semaphores. Data moves between devices by JAX's collectives and lax.ppermute only.
A program may use at most 64 MiB of HBM per device.

v0:
```python
import jax
import jax.numpy as jnp
from jax import lax
from jax.sharding import PartitionSpec as P

epsilon = 1e-06


def normalize_rows(vectors):
    radius = jnp.sqrt(jnp.sum(vectors * vectors, axis=1, keepdims=True) + epsilon)
    return (vectors / radius, radius)


def projection_backward(unit_vectors, radius, gradient):
    inner = jnp.sum(unit_vectors * gradient, axis=1, keepdims=True)
    return (gradient - unit_vectors * inner) / radius


def body(
    request_embeddings,
    frequent_entry_matrix,
    rare_entry_matrix,
    frequent_entry_lines,
    rare_place_parent,
    rare_local_position,
    rare_place_tally,
    sharpness_factor,
    pairscore_additive,
):
    pair_count, row_width = request_embeddings.shape
    owner_total = lax.axis_size("shard")
    slots_cold = rare_place_parent.shape[1]
    capacity = 2 * pair_count * slots_cold // owner_total
    sharpness_multiplier = sharpness_factor[0]
    additive_term = pairscore_additive[0]
    live_slot = jnp.arange(slots_cold)[None, :] < rare_place_tally[:, None]
    live_flat = live_slot.reshape(-1)
    owner_flat = rare_place_parent.reshape(-1)
    owner_onehot = (
        (owner_flat[:, None] == jnp.arange(owner_total)[None, :]) & live_flat[:, None]
    ).astype(jnp.int32)
    rank_before = jnp.cumsum(owner_onehot, axis=0) - owner_onehot
    position = jnp.sum(rank_before * owner_onehot, axis=1)
    dump_slot = owner_total * capacity
    bucket = jnp.where(live_flat, owner_flat * capacity + position, dump_slot)
    requests = (
        jnp.zeros((dump_slot + 1,), jnp.int32).at[bucket].set(rare_local_position.reshape(-1))
    )
    requests = requests[:dump_slot].reshape(owner_total, capacity)
    received = lax.all_to_all(requests, "shard", split_axis=0, concat_axis=0, tiled=True)
    looked = jnp.take(rare_entry_matrix, received, axis=0)
    fetched = lax.all_to_all(looked, "shard", split_axis=0, concat_axis=0, tiled=True)
    fetched_flat = fetched.reshape(dump_slot, row_width)
    picked = jnp.take(fetched_flat, jnp.minimum(bucket, dump_slot - 1), axis=0) * live_flat[
        :, None
    ].astype(jnp.float32)
    cold_sum = jnp.sum(picked.reshape(pair_count, slots_cold, row_width), axis=1)
    hot_index = jnp.arange(frequent_entry_matrix.shape[0])
    hot_counts = jnp.sum(
        (frequent_entry_lines[:, :, None] == hot_index[None, None, :]).astype(jnp.bfloat16), axis=1
    )
    hot_sum = jnp.dot(hot_counts, frequent_entry_matrix, preferred_element_type=jnp.float32)
    candidate_normalized, candidate_norm = normalize_rows(hot_sum + cold_sum)
    request_normalized, request_norm = normalize_rows(request_embeddings.astype(jnp.float32))
    candidate_reduced = candidate_normalized.astype(jnp.bfloat16)
    request_reduced = request_normalized.astype(jnp.bfloat16)
    my_base = lax.axis_index("blk") * pair_count
    target = my_base + jnp.arange(pair_count)
    block_rows = lax.all_gather(candidate_reduced, "blk", axis=0, tiled=True)
    pairwise_scores = (
        sharpness_multiplier
        * lax.dot_general(
            request_reduced,
            block_rows,
            (((1,), (1,)), ((), ())),
            preferred_element_type=jnp.float32,
        )
        + additive_term
    )
    column = jnp.arange(block_rows.shape[0])
    positive = (target[:, None] == column[None, :]).astype(jnp.float32)
    pairscore_derivative = (jax.nn.sigmoid(pairwise_scores) - positive).astype(jnp.bfloat16)
    request_running_total = jnp.dot(
        pairscore_derivative, block_rows, preferred_element_type=jnp.float32
    )
    item_acc = lax.dot_general(
        pairscore_derivative,
        request_reduced,
        (((0,), (0,)), ((), ())),
        preferred_element_type=jnp.float32,
    )
    candidate_portion = lax.psum_scatter(item_acc, "blk", scatter_dimension=0, tiled=True)
    request_derivative = projection_backward(
        request_normalized, request_norm, sharpness_multiplier * request_running_total
    )
    candidate_derivative = projection_backward(
        candidate_normalized, candidate_norm, sharpness_multiplier * candidate_portion
    ).astype(jnp.bfloat16)
    hot_local = lax.dot_general(
        hot_counts,
        candidate_derivative,
        (((0,), (0,)), ((), ())),
        preferred_element_type=jnp.float32,
    )
    slot_grads = jnp.repeat(candidate_derivative, slots_cold, axis=0)
    outgoing = jnp.zeros((dump_slot + 1, row_width), jnp.bfloat16).at[bucket].set(slot_grads)
    outgoing = outgoing[:dump_slot].reshape(owner_total, capacity, row_width)
    incoming = lax.all_to_all(outgoing, "shard", split_axis=0, concat_axis=0, tiled=True)
    cold_local = (
        jnp.zeros((rare_entry_matrix.shape[0], row_width), jnp.float32)
        .at[received.reshape(-1)]
        .add(incoming.reshape(dump_slot, row_width).astype(jnp.float32))
    )
    hot_grad = lax.psum(hot_local, ("shard", "blk"))
    cold_grad = lax.psum_scatter(cold_local, "blk", scatter_dimension=0, tiled=True)
    return (request_derivative, hot_grad, cold_grad)


def solution(mesh):
    in_specs = (
        P(("shard", "blk"), None),
        P(),
        P("shard", None),
        P(("shard", "blk"), None),
        P(("shard", "blk"), None),
        P(("shard", "blk"), None),
        P(("shard", "blk")),
        P(),
        P(),
    )
    out_specs = (P(("shard", "blk"), None), P(), P(("shard", "blk"), None))
    return jax.shard_map(body, mesh=mesh, in_specs=in_specs, out_specs=out_specs, check_vma=False)
```

profile of v0, /device:TPU:8, one launch (start us, length us, event | category | flops | bytes accessed | tf_op | source)
XLA Modules:
  0.0 536.7 jit_solution(4409312277664935398)
XLA Ops:
  7.2 0.8 broadcast_multiply_fusion
  8.0 0.8 copy.72
  8.9 0.7 iota_compare_fusion.4
  9.5 0.8 lt.127
  10.5 0.2 copy.73
  10.7 0.1 lt.133
  11.6 9.0 %reduce-window.6 = s32[32,8,128]{2,1,0:T(8,128)S(1)} reduce-window(s32[32,8,128]{2,1,0:T(8,128)S(1)} %fusion.20, s32[]{:T(128)} %constant.23.clone.1), window={size=1x1x128 pad=0_0x0_0x127_0}, to_apply=%region_2.3 | reduce-window | flops 4161536 | bytes 262148 | tf_op jit(solution)/shard_map/reduce-window
  21.4 4.3 scatter_custom_fusion
  25.9 20.1 %all_to_all.25 = s32[32,1,64]{2,1,0:T(1,128)S(1)} all-to-all(s32[32,1,64]{2,1,0:T(1,128)S(1)} %all_to_all.16), channel_id=1, replica_groups=mesh['shard'=32,'blk'=8] {'shard'}, dimensions={0} | all-to-all | bytes 16384 | tf_op jit(solution)/shard_map/all_to_all | solution.py:50
  46.1 8.6 %gather_fusion = f32[2048,256]{1,0:T(8,128)} fusion(f32[2048,256]{1,0:T(8,128)S(1)} %copy-done, s32[2048]{0:T(1024)S(1)} %broadcast_clamp_fusion), kind=kCustom, calls=%fused_computation | custom fusion | bytes 4202496 | tf_op jit(solution)/shard_map/jit(_take)/gather | solution.py:51
  54.7 3.2 broadcast_select_fusion
  58.0 5.9 %all-to-all-start.1 = ((f32[32,64,256]{2,1,0:T(8,128)}), f32[32,64,256]{2,1,0:T(8,128)}, u32[]{:S(2)}, u32[]{:S(2)}) async-start(f32[32,64,256]{2,1,0:T(8,128)} %broadcast_select_fusion), calls=%async_computation.1 | async-start | bytes 4194304 | tf_op jit(solution)/shard_map/all_to_all | solution.py:52
  64.3 0.8 copy.80
  65.1 1.2 fusion.1
  66.4 44.1 %all-to-all-done.1 = f32[32,64,256]{2,1,0:T(8,128)} async-done(((f32[32,64,256]{2,1,0:T(8,128)}), f32[32,64,256]{2,1,0:T(8,128)}, u32[]{:S(2)}, u32[]{:S(2)}) %all-to-all-start.1) | async-done | bytes 2097184 | tf_op jit(solution)/shard_map/all_to_all | solution.py:52
  110.5 6.3 %gather_fusion.1 = f32[1024,256]{1,0:T(8,128)} fusion(f32[2048,256]{1,0:T(8,128)} %bitcast.9, s32[1024]{0:T(1024)S(1)} %broadcast_clamp_fusion.1), kind=kCustom, calls=%fused_computation.1 | custom fusion | bytes 2101248 | tf_op jit(solution)/shard_map/jit(_take)/gather | solution.py:54
  116.8 2.5 gather.12
  119.3 2.5 multiply_reduce_fusion
  121.8 0.8 copy.85
  122.7 1.8 multiply_reduce_fusion.3
  124.5 0.7 fusion.28
  125.2 0.2 reduce-scatter.3.cloned.1.call-start
  125.4 1.0 copy.71
  127.8 0.6 iota_add_fusion
  128.4 0.6 add_sqrt_fusion.1
  129.0 21.9 %all-gather.2.cloned.1.call-done = bf16[2048,256]{0,1:T(8,128)(2,1)} async-done(((bf16[256,256]{0,1:T(8,128)(2,1)}), bf16[2048,256]{0,1:T(8,128)(2,1)}) %all-gather.2.cloned.1.call-update) | async-done | bytes 1048592 | tf_op jit(solution)/shard_map/all_gather | solution.py:69
  150.9 2.2 fusion.8
  153.1 1.0 copy-done.2
  154.1 1.8 fusion.25
  155.8 37.5 %reduce-scatter.3.cloned.1.call-done = f32[256,256]{0,1:T(8,128)} async-done(((f32[2048,256]{0,1:T(8,128)}), f32[256,256]{0,1:T(8,128)}) %reduce-scatter.3.cloned.1.call-update) | async-done | bytes 262160 | tf_op jit(solution)/shard_map/reduce_scatter | solution.py:92
  193.3 1.0 multiply_reduce_fusion.1
  194.3 1.7 divide_convert_fusion
  196.0 1.0 copy.87
  197.0 0.9 broadcast_in_dim.61
  197.9 2.0 reshape.299
  199.9 6.4 %scatter_custom_fusion.1 = bf16[2049,256]{1,0:T(8,128)(2,1)} fusion(s32[1024]{0:T(1024)} %bitcast.58, bf16[1024,256]{1,0:T(8,128)(2,1)} %reshape.299, bf16[]{:T(256)} %constant.21.clone.1), kind=kCustom, calls=%fused_computation.24 | custom fusion | bytes 1049600 | tf_op jit(solution)/shard_map/scatter | solution.py:106
  206.3 2.3 slice.23
  208.6 10.2 %all-to-all-start.2 = ((bf16[32,64,256]{2,1,0:T(8,128)(2,1)}), bf16[32,64,256]{2,1,0:T(8,128)(2,1)}, u32[]{:S(2)}, u32[]{:S(2)}) async-start(bf16[32,64,256]{2,1,0:T(8,128)(2,1)} %bitcast.48), calls=%async_computation.3 | async-start | bytes 2097152 | tf_op jit(solution)/shard_map/all_to_all | solution.py:108
  218.9 1.8 fusion.29
  220.8 0.5 broadcast.201
  221.3 0.7 reduce.4
  222.1 20.6 %all-to-all-done.2 = bf16[32,64,256]{2,1,0:T(8,128)(2,1)} async-done(((bf16[32,64,256]{2,1,0:T(8,128)(2,1)}), bf16[32,64,256]{2,1,0:T(8,128)(2,1)}, u32[]{:S(2)}, u32[]{:S(2)}) %all-to-all-start.2) | async-done | bytes 1048608 | tf_op jit(solution)/shard_map/all_to_all | solution.py:108
  242.7 15.0 %scatter_custom_fusion.2 = f32[2048,256]{1,0:T(8,128)} fusion(s32[2048]{0:T(1024)S(1)} %bitcast.56, bf16[2048,256]{1,0:T(8,128)(2,1)} %bitcast.15, f32[]{:T(128)} %constant.19.clone.1), kind=kCustom, calls=%fused_computation.16 | custom fusion | flops 1048576 | bytes 3145732 | tf_op jit(solution)/shard_map/scatter-add | solution.py:112
  257.8 1.7 multiply_reduce_fusion.2
  259.6 0.8 copy.88
  260.4 228.4 %all-reduce.2.cloned.1.call-done = f32[2048,256]{1,0:T(8,128)} async-done(((f32[2048,256]{1,0:T(8,128)}), f32[2048,256]{1,0:T(8,128)}) %all-reduce.2.cloned.1.call-update) | async-done | bytes 2097168 | tf_op jit(solution)/shard_map/psum | solution.py:114
  488.9 38.2 %reduce-scatter.5.cloned.1.call-done = f32[256,256]{1,0:T(8,128)} async-done(((f32[2048,256]{1,0:T(8,128)}), f32[256,256]{1,0:T(8,128)}) %reduce-scatter.5.cloned.1.call-update) | async-done | bytes 262160 | tf_op jit(solution)/shard_map/reduce_scatter | solution.py:115
  527.1 3.0 copy.95
  (68 shorter events, 2.7 us)
Async XLA Ops:
  7.2 38.9 %copy-start = (f32[2048,256]{1,0:T(8,128)S(1)}, f32[2048,256]{1,0:T(8,128)}, u32[]{:S(2)}) copy-start(f32[2048,256]{1,0:T(8,128)} %param.11) | copy-start | bytes 6291460
  7.2 13.9 %copy-start.10 = (s32[256,4]{0,1:T(4,128)S(1)}, s32[256,4]{0,1:T(4,128)}, u32[]{:S(2)}) copy-start(s32[256,4]{0,1:T(4,128)} %param.14) | copy-start | bytes 12292
  21.4 33.3 %copy-start.11 = (s32[1024,1]{0,1:T(1,128)}, s32[1024,1]{0,1:T(1,128)S(1)}, u32[]{:S(2)}) copy-start(s32[1024,1]{0,1:T(1,128)S(1)} %get-tuple-element.22) | copy-start | bytes 12292
  58.0 6.2 %copy-start.4 = (s32[256,4]{0,1:T(4,128)S(1)}, s32[256,4]{0,1:T(4,128)}, u32[]{:S(2)}) copy-start(s32[256,4]{0,1:T(4,128)} %param.13) | copy-start | bytes 12292
  58.0 6.2 %copy-start.8 = (s32[256]{0:T(256)S(1)}, s32[256]{0:T(256)}, u32[]{:S(2)}) copy-start(s32[256]{0:T(256)} %param.15) | copy-start | bytes 3076
  58.0 7.2 %copy-start.9 = (s32[256,4]{0,1:T(4,128)S(1)}, s32[256,4]{0,1:T(4,128)}, u32[]{:S(2)}) copy-start(s32[256,4]{0,1:T(4,128)} %param.12) | copy-start | bytes 12292
  58.0 52.5 %all-to-all-start.1 = ((f32[32,64,256]{2,1,0:T(8,128)}), f32[32,64,256]{2,1,0:T(8,128)}, u32[]{:S(2)}, u32[]{:S(2)}) async-start(f32[32,64,256]{2,1,0:T(8,128)} %broadcast_select_fusion), calls=%async_computation.1 | async-start | bytes 4194304 | tf_op jit(solution)/shard_map/all_to_all | solution.py:52
  63.9 87.0 %all-gather.2.cloned.1.call-start = ((), (), s32[]{:S(2)}) async-start(), calls=%async_computation.5 | async-start | bytes 1179648 | tf_op jit(solution)/shard_map/all_gather | solution.py:69
  124.5 0.9 copy-start.5
  125.2 68.1 %reduce-scatter.3.cloned.1.call-start = ((), (), s32[]{:S(2)}) async-start(), calls=%async_computation.6 | async-start | bytes 2359296 | tf_op jit(solution)/shard_map/reduce_scatter | solution.py:92
  150.9 3.2 copy-start.6
  153.0 1.0 copy-start.2
  206.3 12.6 %copy-start.1 = (bf16[256,256]{0,1:T(8,128)(2,1)S(1)}, bf16[256,256]{0,1:T(8,128)(2,1)}, u32[]{:S(2)}) copy-start(bf16[256,256]{0,1:T(8,128)(2,1)} %divide_convert_fusion) | copy-start | bytes 393220
  208.6 34.1 %all-to-all-start.2 = ((bf16[32,64,256]{2,1,0:T(8,128)(2,1)}), bf16[32,64,256]{2,1,0:T(8,128)(2,1)}, u32[]{:S(2)}, u32[]{:S(2)}) async-start(bf16[32,64,256]{2,1,0:T(8,128)(2,1)} %bitcast.48), calls=%async_computation.3 | async-start | bytes 2097152 | tf_op jit(solution)/shard_map/all_to_all | solution.py:108
  218.9 270.0 %all-reduce.2.cloned.1.call-start = ((), (), s32[]{:S(2)}) async-start(), calls=%async_computation.7 | async-start | bytes 4194304 | tf_op jit(solution)/shard_map/psum | solution.py:114
  220.8 306.4 %reduce-scatter.5.cloned.1.call-start = ((), (), s32[]{:S(2)}) async-start(), calls=%async_computation.8 | async-start | bytes 2359296 | tf_op jit(solution)/shard_map/reduce_scatter | solution.py:115
  242.7 15.1 %copy-start.3 = (bf16[256,2048]{1,0:T(8,128)(2,1)S(1)}, bf16[256,2048]{1,0:T(8,128)(2,1)}, u32[]{:S(2)}) copy-start(bf16[256,2048]{1,0:T(8,128)(2,1)} %copy-done.2) | copy-start | bytes 3145732
  242.7 15.1 %copy-start.7 = (f32[256]{0:T(256)S(1)}, f32[256]{0:T(256)}, u32[]{:S(2)}) copy-start(f32[256]{0:T(256)} %add_sqrt_fusion.1) | copy-start | bytes 3076
Sparse Core Ops, SparseCore 0:
  125.3 25.5 all-gather.1
  156.0 37.3 reduce-scatter.2
  225.6 263.2 all-reduce.1
  491.9 35.2 reduce-scatter.4
where the time goes:
time: 538 us; the launch traced here: 537 us
  waiting for transfers between devices  391 us (73%)
  local copies, waits for them, and re-layouts  46.3 us (9%)
  other arithmetic  38.2 us (7%)
  blocking collectives  20.1 us (4%)
  starting transfers between devices  16.5 us (3%)
  between operations  15.4 us (3%)
  matrix products  9.24 us (2%)
    psum x1, waiting for transfers between devices, body(): hot_grad = lax.psum(hot_local, ('shard', 'blk'))  228 us
    all_to_all x1, waiting for transfers between devices, body(): lax.all_to_all(looked, 'shard', split_axis=0, concat_axis=0, tiled=True)  44.1 us
    reduce_scatter x1, waiting for transfers between devices, body(): lax.psum_scatter(cold_local, 'blk', scatter_dimension=0, tiled=True)  38.2 us
    reduce_scatter x1, waiting for transfers between devices, body(): lax.psum_scatter(item_acc, 'blk', scatter_dimension=0, tiled=True)  37.5 us
    all_gather x1, waiting for transfers between devices, body(): block_rows = lax.all_gather(candidate_reduced, 'blk', axis=0, tiled=True)  21.9 us
    all_to_all x1, waiting for transfers between devices, body(): lax.all_to_all(outgoing, 'shard', split_axis=0, concat_axis=0, tiled=True)  20.6 us
    all_to_all x1, blocking collectives, body(): lax.all_to_all(requests, 'shard', split_axis=0, concat_axis=0, tiled=True)  20.1 us
    scatter-add x1, other arithmetic, body(): cold_local = jnp.zeros((rare_entry_matrix.shape[0], row_width), jnp.float...  15 us
  transfers between devices with their start and end apart: 6, of which 6 were waited for; matrix products, arithmetic and copies ran while one was open for 5% of the time, Pallas kernels for 0%

commit v1 on v0

--- a/solution.py
+++ b/solution.py
@@ -111,7 +111,7 @@
         .at[received.reshape(-1)]
         .add(incoming.reshape(dump_slot, row_width).astype(jnp.float32))
     )
-    hot_grad = lax.psum(hot_local, ("shard", "blk"))
+    hot_grad = lax.psum(lax.psum(hot_local, "blk"), "shard")
     cold_grad = lax.psum_scatter(cold_local, "blk", scatter_dimension=0, tiled=True)
     return (request_derivative, hot_grad, cold_grad)
 

time: 538 us -> 487 us (0.905)
  waiting for transfers between devices: 391 us -> 344 us
    psum x1 -> x2, waiting for transfers between devices: 228 us -> 170 us  [body(): hot_grad = lax.psum(lax.psum(hot_local, 'blk'), 'shard')]
    all_to_all x1, waiting for transfers between devices: 20.6 us -> 32.7 us  [body(): lax.all_to_all(outgoing, 'shard', split_axis=0, concat_axis=0, tiled=True)]
  transfers between devices with their start and end apart: 6 -> 7, of which waited for: 6 -> 7; matrix products, arithmetic and copies ran while one was open for 5% -> 6% of each run, Pallas kernels for 0% -> 0%
where the time goes in v1:
time: 487 us; the launch traced here: 486 us
  waiting for transfers between devices  344 us (71%)
  local copies, waits for them, and re-layouts  43.4 us (9%)
  other arithmetic  37.2 us (8%)
  blocking collectives  20.1 us (4%)
  starting transfers between devices  16.5 us (3%)
  between operations  15.4 us (3%)
  matrix products  9.24 us (2%)
    psum x2, waiting for transfers between devices, body(): hot_grad = lax.psum(lax.psum(hot_local, 'blk'), 'shard')  170 us
    all_to_all x1, waiting for transfers between devices, body(): lax.all_to_all(looked, 'shard', split_axis=0, concat_axis=0, tiled=True)  44.1 us
    reduce_scatter x1, waiting for transfers between devices, body(): lax.psum_scatter(cold_local, 'blk', scatter_dimension=0, tiled=True)  38 us
    reduce_scatter x1, waiting for transfers between devices, body(): lax.psum_scatter(item_acc, 'blk', scatter_dimension=0, tiled=True)  37.4 us
    all_to_all x1, waiting for transfers between devices, body(): lax.all_to_all(outgoing, 'shard', split_axis=0, concat_axis=0, tiled=True)  32.7 us
    all_gather x1, waiting for transfers between devices, body(): block_rows = lax.all_gather(candidate_reduced, 'blk', axis=0, tiled=True)  22.2 us
    all_to_all x1, blocking collectives, body(): lax.all_to_all(requests, 'shard', split_axis=0, concat_axis=0, tiled=True)  20.1 us
    scatter-add x1, other arithmetic, body(): cold_local = jnp.zeros((rare_entry_matrix.shape[0], row_width), jnp.float...  14.8 us
  transfers between devices with their start and end apart: 7, of which 7 were waited for; matrix products, arithmetic and copies ran while one was open for 6% of the time, Pallas kernels for 0%

profile of v1, /device:TPU:8, one launch (start us, length us, event | category | flops | bytes accessed | tf_op | source)
XLA Modules:
  0.0 486.0 jit_solution(14983052827430565342)
XLA Ops:
  7.2 0.8 broadcast_multiply_fusion
  8.0 0.8 copy.72
  8.9 0.7 iota_compare_fusion.4
  9.5 0.8 lt.127
  10.5 0.2 copy.73
  11.6 9.0 %reduce-window.6 = s32[32,8,128]{2,1,0:T(8,128)S(1)} reduce-window(s32[32,8,128]{2,1,0:T(8,128)S(1)} %fusion.20, s32[]{:T(128)} %constant.23.clone.1), window={size=1x1x128 pad=0_0x0_0x127_0}, to_apply=%region_2.3 | reduce-window | flops 4161536 | bytes 262148 | tf_op jit(solution)/shard_map/reduce-window
  21.4 4.3 scatter_custom_fusion
  25.9 20.1 %all_to_all.25 = s32[32,1,64]{2,1,0:T(1,128)S(1)} all-to-all(s32[32,1,64]{2,1,0:T(1,128)S(1)} %all_to_all.16), channel_id=1, replica_groups=mesh['shard'=32,'blk'=8] {'shard'}, dimensions={0} | all-to-all | bytes 16384 | tf_op jit(solution)/shard_map/all_to_all | solution.py:50
  46.1 8.6 %gather_fusion = f32[2048,256]{1,0:T(8,128)} fusion(f32[2048,256]{1,0:T(8,128)S(1)} %copy-done, s32[2048]{0:T(1024)S(1)} %broadcast_clamp_fusion), kind=kCustom, calls=%fused_computation | custom fusion | bytes 4202496 | tf_op jit(solution)/shard_map/jit(_take)/gather | solution.py:51
  54.7 3.2 broadcast_select_fusion
  58.0 5.9 %all-to-all-start.1 = ((f32[32,64,256]{2,1,0:T(8,128)}), f32[32,64,256]{2,1,0:T(8,128)}, u32[]{:S(2)}, u32[]{:S(2)}) async-start(f32[32,64,256]{2,1,0:T(8,128)} %broadcast_select_fusion), calls=%async_computation.1 | async-start | bytes 4194304 | tf_op jit(solution)/shard_map/all_to_all | solution.py:52
  64.3 0.8 copy.80
  65.1 1.2 fusion.1
  66.4 44.1 %all-to-all-done.1 = f32[32,64,256]{2,1,0:T(8,128)} async-done(((f32[32,64,256]{2,1,0:T(8,128)}), f32[32,64,256]{2,1,0:T(8,128)}, u32[]{:S(2)}, u32[]{:S(2)}) %all-to-all-start.1) | async-done | bytes 2097184 | tf_op jit(solution)/shard_map/all_to_all | solution.py:52
  110.5 6.3 %gather_fusion.1 = f32[1024,256]{1,0:T(8,128)} fusion(f32[2048,256]{1,0:T(8,128)} %bitcast.9, s32[1024]{0:T(1024)S(1)} %broadcast_clamp_fusion.1), kind=kCustom, calls=%fused_computation.1 | custom fusion | bytes 2101248 | tf_op jit(solution)/shard_map/jit(_take)/gather | solution.py:54
  116.8 2.5 gather.12
  119.3 2.5 multiply_reduce_fusion
  121.8 0.8 copy.85
  122.7 1.8 multiply_reduce_fusion.3
  124.5 0.7 fusion.28
  125.3 1.0 copy.71
  127.6 0.6 iota_add_fusion
  128.2 0.5 add_sqrt_fusion.1
  128.7 22.2 %all-gather.2.cloned.1.call-done = bf16[2048,256]{0,1:T(8,128)(2,1)} async-done(((bf16[256,256]{0,1:T(8,128)(2,1)}), bf16[2048,256]{0,1:T(8,128)(2,1)}) %all-gather.2.cloned.1.call-update) | async-done | bytes 1048592 | tf_op jit(solution)/shard_map/all_gather | solution.py:69
  150.9 2.2 fusion.8
  153.1 1.0 copy-done.3
  154.1 1.8 fusion.25
  155.9 37.4 %reduce-scatter.3.cloned.1.call-done = f32[256,256]{0,1:T(8,128)} async-done(((f32[2048,256]{0,1:T(8,128)}), f32[256,256]{0,1:T(8,128)}) %reduce-scatter.3.cloned.1.call-update) | async-done | bytes 262160 | tf_op jit(solution)/shard_map/reduce_scatter | solution.py:92
  193.3 1.0 multiply_reduce_fusion.1
  194.3 1.0 divide_convert_fusion
  195.4 0.6 copy-done.1
  196.0 1.8 fusion.29
  197.8 0.2 all-reduce.5.cloned.1.call-start
  198.1 69.6 %all-reduce.3.cloned.1.call-done = f32[2048,256]{1,0:T(8,128)} async-done(((f32[2048,256]{1,0:T(8,128)}), f32[2048,256]{1,0:T(8,128)}) %all-reduce.3.cloned.1.call-update) | async-done | bytes 2097168 | tf_op jit(solution)/shard_map/psum | solution.py:114
  267.9 0.9 reshape.299
  268.8 5.6 %scatter_custom_fusion.1 = bf16[2049,256]{1,0:T(8,128)(2,1)S(1)} fusion(s32[1024]{0:T(1024)} %bitcast.59, bf16[1024,256]{1,0:T(8,128)(2,1)} %reshape.299, bf16[]{:T(256)} %constant.21.clone.1), kind=kCustom, calls=%fused_computation.24 | custom fusion | bytes 1049600 | tf_op jit(solution)/shard_map/scatter | solution.py:106
  274.5 1.0 slice.23
  275.5 10.2 %all-to-all-start.2 = ((bf16[32,64,256]{2,1,0:T(8,128)(2,1)}), bf16[32,64,256]{2,1,0:T(8,128)(2,1)S(1)}, u32[]{:S(2)}, u32[]{:S(2)}) async-start(bf16[32,64,256]{2,1,0:T(8,128)(2,1)} %bitcast.49), calls=%async_computation.3 | async-start | bytes 2097152 | tf_op jit(solution)/shard_map/all_to_all | solution.py:108
  285.7 0.5 broadcast.201
  286.2 0.7 reduce.4
  287.0 32.7 %all-to-all-done.2 = bf16[32,64,256]{2,1,0:T(8,128)(2,1)S(1)} async-done(((bf16[32,64,256]{2,1,0:T(8,128)(2,1)}), bf16[32,64,256]{2,1,0:T(8,128)(2,1)S(1)}, u32[]{:S(2)}, u32[]{:S(2)}) %all-to-all-start.2) | async-done | bytes 1048608 | tf_op jit(solution)/shard_map/all_to_all | solution.py:108
  319.8 14.8 %scatter_custom_fusion.2 = f32[2048,256]{1,0:T(8,128)} fusion(s32[2048]{0:T(1024)S(1)} %bitcast.57, bf16[2048,256]{1,0:T(8,128)(2,1)S(1)} %bitcast.48, f32[]{:T(128)} %constant.19.clone.1), kind=kCustom, calls=%fused_computation.16 | custom fusion | flops 1048576 | bytes 3145732 | tf_op jit(solution)/shard_map/scatter-add | solution.py:112
  334.6 1.2 copy-done.4
  335.8 1.7 multiply_reduce_fusion.2
  337.6 0.8 copy.88
  338.4 100.0 %all-reduce.5.cloned.1.call-done = f32[2048,256]{1,0:T(8,128)} async-done(((f32[2048,256]{1,0:T(8,128)}), f32[2048,256]{1,0:T(8,128)}) %all-reduce.5.cloned.1.call-update) | async-done | bytes 2097168 | tf_op jit(solution)/shard_map/psum | solution.py:114
  438.4 38.0 %reduce-scatter.5.cloned.1.call-done = f32[256,256]{1,0:T(8,128)} async-done(((f32[2048,256]{1,0:T(8,128)}), f32[256,256]{1,0:T(8,128)}) %reduce-scatter.5.cloned.1.call-update) | async-done | bytes 262160 | tf_op jit(solution)/shard_map/reduce_scatter | solution.py:115
  476.4 3.0 copy.96
  (73 shorter events, 3.1 us)
Async XLA Ops:
  7.2 38.9 %copy-start = (f32[2048,256]{1,0:T(8,128)S(1)}, f32[2048,256]{1,0:T(8,128)}, u32[]{:S(2)}) copy-start(f32[2048,256]{1,0:T(8,128)} %param.11) | copy-start | bytes 6291460
  7.2 13.9 %copy-start.11 = (s32[256,4]{0,1:T(4,128)S(1)}, s32[256,4]{0,1:T(4,128)}, u32[]{:S(2)}) copy-start(s32[256,4]{0,1:T(4,128)} %param.14) | copy-start | bytes 12292
  21.4 33.3 %copy-start.12 = (s32[1024,1]{0,1:T(1,128)}, s32[1024,1]{0,1:T(1,128)S(1)}, u32[]{:S(2)}) copy-start(s32[1024,1]{0,1:T(1,128)S(1)} %get-tuple-element.22) | copy-start | bytes 12292
  58.0 6.2 %copy-start.5 = (s32[256,4]{0,1:T(4,128)S(1)}, s32[256,4]{0,1:T(4,128)}, u32[]{:S(2)}) copy-start(s32[256,4]{0,1:T(4,128)} %param.13) | copy-start | bytes 12292
  58.0 6.2 %copy-start.9 = (s32[256]{0:T(256)S(1)}, s32[256]{0:T(256)}, u32[]{:S(2)}) copy-start(s32[256]{0:T(256)} %param.15) | copy-start | bytes 3076
  58.0 7.2 %copy-start.10 = (s32[256,4]{0,1:T(4,128)S(1)}, s32[256,4]{0,1:T(4,128)}, u32[]{:S(2)}) copy-start(s32[256,4]{0,1:T(4,128)} %param.12) | copy-start | bytes 12292
  58.0 52.5 %all-to-all-start.1 = ((f32[32,64,256]{2,1,0:T(8,128)}), f32[32,64,256]{2,1,0:T(8,128)}, u32[]{:S(2)}, u32[]{:S(2)}) async-start(f32[32,64,256]{2,1,0:T(8,128)} %broadcast_select_fusion), calls=%async_computation.1 | async-start | bytes 4194304 | tf_op jit(solution)/shard_map/all_to_all | solution.py:52
  63.9 87.0 %all-gather.2.cloned.1.call-start = ((), (), s32[]{:S(2)}) async-start(), calls=%async_computation.5 | async-start | bytes 1179648 | tf_op jit(solution)/shard_map/all_gather | solution.py:69
  124.5 0.8 copy-start.6
  125.2 68.1 %reduce-scatter.3.cloned.1.call-start = ((), (), s32[]{:S(2)}) async-start(), calls=%async_computation.6 | async-start | bytes 2359296 | tf_op jit(solution)/shard_map/reduce_scatter | solution.py:92
  150.9 3.2 copy-start.7
  153.0 1.0 copy-start.3
  155.8 111.8 %all-reduce.3.cloned.1.call-start = ((), (), s32[]{:S(2)}) async-start(), calls=%async_computation.7 | async-start | bytes 4194304 | tf_op jit(solution)/shard_map/psum | solution.py:114
  195.3 0.7 copy-start.1
  197.8 69.8 %copy-start.2 = (bf16[256,256]{0,1:T(8,128)(2,1)S(1)}, bf16[256,256]{0,1:T(8,128)(2,1)}, u32[]{:S(2)}) copy-start(bf16[256,256]{0,1:T(8,128)(2,1)} %copy-done.1) | copy-start | bytes 393220
  197.8 240.6 %all-reduce.5.cloned.1.call-start = ((), (), s32[]{:S(2)}) async-start(), calls=%async_computation.8 | async-start | bytes 4194304 | tf_op jit(solution)/shard_map/psum | solution.py:114
  275.5 44.2 %all-to-all-start.2 = ((bf16[32,64,256]{2,1,0:T(8,128)(2,1)}), bf16[32,64,256]{2,1,0:T(8,128)(2,1)S(1)}, u32[]{:S(2)}, u32[]{:S(2)}) async-start(bf16[32,64,256]{2,1,0:T(8,128)(2,1)} %bitcast.49), calls=%async_computation.3 | async-start | bytes 2097152 | tf_op jit(solution)/shard_map/all_to_all | solution.py:108
  285.7 190.7 %reduce-scatter.5.cloned.1.call-start = ((), (), s32[]{:S(2)}) async-start(), calls=%async_computation.9 | async-start | bytes 2359296 | tf_op jit(solution)/shard_map/reduce_scatter | solution.py:115
  319.8 14.8 %copy-start.8 = (f32[256]{0:T(256)S(1)}, f32[256]{0:T(256)}, u32[]{:S(2)}) copy-start(f32[256]{0:T(256)} %add_sqrt_fusion.1) | copy-start | bytes 3076
  334.6 1.2 copy-start.4
Sparse Core Ops, SparseCore 0:
  125.3 25.5 all-gather.1
  156.0 37.3 reduce-scatter.2
  198.0 69.6 all-reduce.2
  271.0 167.3 all-reduce.4
  441.4 35.0 reduce-scatter.4
